TPU v7x, 256 devices: a whole 4x4x8 slice. The times are simulated.
256 devices in a mesh: aux: 8 (over x_lo, y), occ: 32 (over x_hi, z, core).
Axes of the slice: x: 4 (x_hi: 2, x_lo: 2; x = x_hi * 2 + x_lo), y: 4, z: 8, core: 2. Of those that a mesh axis runs over, the one named last changes fastest.
Arguments:
- factor: bfloat16 [6144, 32, 1536], P('aux', 'occ'), may hold values from -0.67578125 to 0.67578125
- occ_energy: float32 [1024], replicated, may hold values from -3 to -0.5
- vir_energy: float32 [3072], replicated, may hold values from 0.5 to 4
- occ_pick: int32 [32], replicated, may hold values from 0 to 1023
- vir_pick: int32 [1536], replicated, may hold values from 0 to 3071
Outputs:
- gamma: float32 [6144, 32, 1536], P('aux', 'occ')
All inputs are finite; a program needn't handle non-finite values.
Results may differ from a plain program's by a relative error of at most 0.0024.
Values may be sent and summed in bfloat16 or wider, within the bound.
A program may use at most 192 MiB of HBM per device.

v0:
```python
import jax
import jax.numpy as jnp
from jax import lax
from jax.sharding import PartitionSpec as P


def shifted(block, axis, distance):
    devices = range(lax.axis_size(axis))
    route = [((i - distance) % len(devices), i) for i in devices]
    return lax.ppermute(block, axis, route)


def pair_density(left_block, right_block, pair_level, vir_levels, vir_rows):
    integrals = lax.psum_scatter(
        lax.dot_general(
            right_block, left_block, (((0,), (0,)), ((), ())), preferred_element_type=jnp.float32
        ),
        "aux",
        scatter_dimension=0,
        tiled=True,
    )
    divisor = pair_level - vir_rows[:, None] - vir_levels[None, :]
    amplitudes = (integrals / divisor).astype(jnp.bfloat16)
    return jnp.dot(
        right_block,
        lax.all_gather(amplitudes, "aux", axis=0, tiled=True),
        preferred_element_type=jnp.float32,
    )


def on_device(factor, occ_energy, vir_energy, occ_pick, vir_pick):
    aux_count = lax.axis_size("aux")
    occ_count = lax.axis_size("occ")
    aux_place = lax.axis_index("aux")
    occ_place = lax.axis_index("occ")
    local_occ = factor.shape[1]
    virtuals = factor.shape[2]
    row_count = virtuals // aux_count
    occ_levels = jnp.take(occ_energy, occ_pick)
    vir_levels = jnp.take(vir_energy, vir_pick)
    row_start = aux_place * row_count
    vir_rows = lax.dynamic_slice_in_dim(vir_levels, row_start, row_count)
    near_block = shifted(factor, "occ", 1)
    far_block = shifted(near_block, "occ", 1)
    partners = ((1, near_block), (2, far_block))
    left_block = factor[:, 0, :]
    own_level = lax.dynamic_index_in_dim(occ_levels, occ_place * local_occ + 0, keepdims=False)
    density = jnp.zeros((factor.shape[0], virtuals), jnp.float32)
    for distance, block in partners:
        source_base = (occ_place - distance) % occ_count * local_occ
        right_block = block[:, 0, :]
        other_level = lax.dynamic_index_in_dim(occ_levels, source_base + 0, keepdims=False)
        density = density + pair_density(
            left_block, right_block, own_level + other_level, vir_levels, vir_rows
        )
    results = [density]
    return jnp.stack(results, axis=1)


def solution(mesh):
    placed = (P("aux", "occ", None), P(), P(), P(), P())
    return jax.shard_map(
        on_device, mesh=mesh, in_specs=placed, out_specs=P("aux", "occ", None), check_vma=False
    )
```

profile of v0, /device:TPU:1, one launch (start us, length us, event | category | flops | bytes accessed | tf_op | source)
XLA Modules:
  0.0 427.4 jit_solution(7457580632704250876)
XLA Ops:
  6.5 0.0 copy-start
  6.5 0.0 reduce-scatter.3.cloned.1.call-start
  6.5 3.0 collective-permute-start
  9.6 26.1 %collective-permute-done = bf16[768,1,1536]{2,0,1:T(8,128)(2,1)S(1)} collective-permute-done((bf16[768,1,1536]{2,0,1:T(8,128)(2,1)}, bf16[768,1,1536]{2,0,1:T(8,128)(2,1)S(1)}, u32[]{:S(2)}, u32[]{:S(2)}) %collective-permute-start) | collective-permute-done | bytes 2359328 | tf_op jit(solution)/shard_map/ppermute | solution.py:10
  35.7 0.0 copy-start.4
  35.7 1.4 copy-done.4
  37.1 7.9 %fusion.4 = f32[1536,1536]{1,0:T(8,128)} fusion(bf16[768,1,1536]{2,0,1:T(8,128)(2,1)} %param.5, bf16[768,1,1536]{2,0,1:T(8,128)(2,1)S(1)} %collective-permute-done), kind=kOutput, calls=%fused_computation.7 | convolution fusion | flops 3623878656 | bytes 14155776 | tf_op jit(solution)/shard_map/dot_general | solution.py:15
  45.0 0.0 copy-start.3
  45.0 0.0 reduce-scatter.3.cloned.1.call-update
  45.0 0.0 reduce-scatter.5.cloned.1.call-start
  45.1 2.5 collective-permute-start.1
  47.5 26.1 %collective-permute-done.1 = bf16[768,1,1536]{2,0,1:T(8,128)(2,1)S(1)} collective-permute-done((bf16[768,1,1536]{2,0,1:T(8,128)(2,1)}, bf16[768,1,1536]{2,0,1:T(8,128)(2,1)S(1)}, u32[]{:S(2)}, u32[]{:S(2)}) %collective-permute-start.1) | collective-permute-done | bytes 2359328 | tf_op jit(solution)/shard_map/ppermute | solution.py:10
  73.7 0.0 copy-start.6
  73.7 1.4 copy-done.6
  75.1 0.0 copy-done.3
  75.1 6.3 %fusion.1 = f32[1536,1536]{1,0:T(8,128)} fusion(bf16[768,1,1536]{2,0,1:T(8,128)(2,1)S(1)} %collective-permute-done.1, bf16[768,1,1536]{2,0,1:T(8,128)(2,1)S(1)} %copy-done.3), kind=kOutput, calls=%fused_computation.4 | convolution fusion | flops 3623878656 | bytes 14155776 | tf_op jit(solution)/shard_map/dot_general | solution.py:15
  81.4 0.0 copy-start.7
  81.4 0.0 copy-start.1
  81.4 0.0 copy-start.2
  81.4 0.0 reduce-scatter.5.cloned.1.call-update
  81.4 0.0 all-gather.3.cloned.1.call-start
  81.5 0.5 copy-done.7
  82.0 0.0 copy-done.1
  82.1 0.7 gather_fusion
  82.7 0.7 fusion.9
  86.1 0.0 copy-done.2
  86.1 0.0 copy-done
  86.1 8.4 %gather_fusion.1 = f32[1536]{0:T(1024)S(1)} fusion(f32[3072]{0:T(1024)S(1)} %copy-done, s32[2048]{0:T(1024)S(1)} %pad_clamp_fusion), kind=kCustom, calls=%fused_computation.1 | custom fusion | bytes 18432 | tf_op jit(solution)/shard_map/jit(_take)/gather | solution.py:40
  94.5 0.1 dynamic-slice_subtract_fusion
  94.6 80.0 %reduce-scatter.3.cloned.1.call-done = f32[192,1536]{1,0:T(8,128)} async-done(((f32[1536,1536]{1,0:T(8,128)}), f32[192,1536]{1,0:T(8,128)}) %reduce-scatter.3.cloned.1.call-update) | async-done | bytes 1179664 | tf_op jit(solution)/shard_map/reduce_scatter | solution.py:14
  174.6 100.9 %reduce-scatter.5.cloned.1.call-done = f32[192,1536]{1,0:T(8,128)} async-done(((f32[1536,1536]{1,0:T(8,128)}), f32[192,1536]{1,0:T(8,128)}) %reduce-scatter.5.cloned.1.call-update) | async-done | bytes 1179664 | tf_op jit(solution)/shard_map/reduce_scatter | solution.py:14
  275.5 0.0 copy-start.5
  275.5 3.2 divide_convert_fusion
  278.7 0.0 all-gather.3.cloned.1.call-update
  278.7 0.2 all-gather.5.cloned.1.call-start
  279.0 0.3 all-gather.5.cloned.1.call-update
  279.3 58.4 %all-gather.3.cloned.1.call-done = bf16[1536,1536]{1,0:T(8,128)(2,1)} async-done(((bf16[192,1536]{1,0:T(8,128)(2,1)}), bf16[1536,1536]{1,0:T(8,128)(2,1)}) %all-gather.3.cloned.1.call-update) | async-done | bytes 4718608 | tf_op jit(solution)/shard_map/all_gather | solution.py:26
  337.7 0.0 copy-done.5
  337.7 8.4 %fusion.6 = f32[1536,768]{1,0:T(8,128)} fusion(bf16[1536,1536]{1,0:T(8,128)(2,1)} %all-gather.3.cloned.1.call-done, bf16[768,1,1536]{2,0,1:T(8,128)(2,1)S(1)} %copy-done.5), kind=kOutput, calls=%fused_computation.9 | convolution fusion | flops 3623878656 | bytes 11796480 | tf_op jit(solution)/shard_map/dot_general | solution.py:24
  346.2 52.1 %all-gather.5.cloned.1.call-done = bf16[1536,1536]{1,0:T(8,128)(2,1)} async-done(((bf16[192,1536]{1,0:T(8,128)(2,1)}), bf16[1536,1536]{1,0:T(8,128)(2,1)}) %all-gather.5.cloned.1.call-update) | async-done | bytes 4718608 | tf_op jit(solution)/shard_map/all_gather | solution.py:26
  398.3 10.5 %add_bitcast_fusion = f32[768,1,1536]{0,2,1:T(8,128)} fusion(f32[1536,768]{1,0:T(8,128)} %fusion.6, bf16[1536,1536]{1,0:T(8,128)(2,1)} %all-gather.5.cloned.1.call-done, bf16[768,1,1536]{2,0,1:T(8,128)(2,1)} %copy-done.6), kind=kOutput, calls=%fused_computation.2 | convolution fusion | flops 3625058304 | bytes 16515072 | tf_op jit(solution)/shard_map/dot_general | solution.py:24
  408.8 12.1 %copy.7 = f32[768,1,1536]{2,1,0:T(1,128)} copy(f32[768,1,1536]{0,2,1:T(8,128)} %add_bitcast_fusion) | data formatting | bytes 9437184 | tf_op jit(solution)/shard_map/stack | solution.py:57
  (6 shorter events, 0.0 us)
Async XLA Ops:
  6.5 79.6 %copy-start = (f32[3072]{0:T(1024)S(1)}, f32[3072]{0:T(1024)}, u32[]{:S(2)}) copy-start(f32[3072]{0:T(1024)} %param.7) | copy-start | bytes 36868
  6.5 168.1 %reduce-scatter.3.cloned.1.call-start = ((), (), s32[]{:S(2)}) async-start(), calls=%async_computation.2 | async-start | bytes 10616832 | tf_op jit(solution)/shard_map/reduce_scatter | solution.py:14
  6.5 29.1 %collective-permute-start = (bf16[768,1,1536]{2,0,1:T(8,128)(2,1)}, bf16[768,1,1536]{2,0,1:T(8,128)(2,1)S(1)}, u32[]{:S(2)}, u32[]{:S(2)}) collective-permute-start(bf16[768,1,1536]{2,0,1:T(8,128)(2,1)} %param.5), channel_id=1, source_target_pairs={{31,0},{0,1},{1,2},{2,3},{3,4},{4,5},{5,6},{6,7},{7,8},{8,9},{9,10... | collective-permute-start | bytes 7077896 | tf_op jit(solution)/shard_map/ppermute | solution.py:10
  35.7 1.4 copy-start.4
  45.0 30.0 %copy-start.3 = (bf16[768,1,1536]{2,0,1:T(8,128)(2,1)S(1)}, bf16[768,1,1536]{2,0,1:T(8,128)(2,1)}, u32[]{:S(2)}) copy-start(bf16[768,1,1536]{2,0,1:T(8,128)(2,1)} %param.5) | copy-start | bytes 7077892
  45.0 230.5 %reduce-scatter.5.cloned.1.call-start = ((), (), s32[]{:S(2)}) async-start(), calls=%async_computation.4 | async-start | bytes 10616832 | tf_op jit(solution)/shard_map/reduce_scatter | solution.py:14
  45.1 28.6 %collective-permute-start.1 = (bf16[768,1,1536]{2,0,1:T(8,128)(2,1)}, bf16[768,1,1536]{2,0,1:T(8,128)(2,1)S(1)}, u32[]{:S(2)}, u32[]{:S(2)}) collective-permute-start(bf16[768,1,1536]{2,0,1:T(8,128)(2,1)} %copy-done.4), channel_id=1, source_target_pairs={{31,0},{0,1},{1,2},{2,3},{3,4},{4,5},{5,6},{6,7},{7,8},{8,9},{9,10... | collective-permute-start | bytes 7077896 | tf_op jit(solution)/shard_map/ppermute | solution.py:10
  73.7 1.4 copy-start.6
  81.4 0.7 copy-start.7
  81.4 0.7 copy-start.1
  81.4 4.7 %copy-start.2 = (s32[1536]{0:T(1024)S(1)}, s32[1536]{0:T(1024)}, u32[]{:S(2)}) copy-start(s32[1536]{0:T(1024)} %param.9) | copy-start | bytes 18436
  81.4 256.3 %all-gather.3.cloned.1.call-start = ((), (), s32[]{:S(2)}) async-start(), calls=%async_computation.3 | async-start | bytes 5308416 | tf_op jit(solution)/shard_map/all_gather | solution.py:26
  275.5 62.2 %copy-start.5 = (bf16[768,1,1536]{2,0,1:T(8,128)(2,1)S(1)}, bf16[768,1,1536]{2,0,1:T(8,128)(2,1)}, u32[]{:S(2)}) copy-start(bf16[768,1,1536]{2,0,1:T(8,128)(2,1)} %copy-done.4) | copy-start | bytes 7077892
  278.7 119.5 %all-gather.5.cloned.1.call-start = ((), (), s32[]{:S(2)}) async-start(), calls=%async_computation.5 | async-start | bytes 5308416 | tf_op jit(solution)/shard_map/all_gather | solution.py:26
Sparse Core Ops, SparseCore 0:
  45.2 129.3 reduce-scatter.2
  177.1 98.3 reduce-scatter.4
  278.9 58.8 all-gather.2
  339.4 58.8 all-gather.4
where the time goes:
time: 428 us; the launch traced here: 427 us
  waiting for transfers between devices  344 us (80%)
  matrix products  33.2 us (8%)
  local copies, waits for them, and re-layouts  25.2 us (6%)
  between operations  15.9 us (4%)
  starting transfers between devices  5.79 us (1%)
    reduce_scatter x2, waiting for transfers between devices, pair_density(): lax.psum_scatter(lax.dot_general(right_block, left_block, (((0,), (0,)),...  181 us
    all_gather x2, waiting for transfers between devices, pair_density(): lax.all_gather(amplitudes, 'aux', axis=0, tiled=True)  110 us
    ppermute x2, waiting for transfers between devices, shifted(): return lax.ppermute(block, axis, route)  52.2 us
    dot_general x2, matrix products, pair_density(): jnp.dot(right_block, lax.all_gather(amplitudes, 'aux', axis=0, tiled=True...  18.9 us
    dot_general x2, matrix products, pair_density(): lax.dot_general(right_block, left_block, (((0,), (0,)), ((), ())), prefer...  14.2 us
    another operation x1, local copies, waits for them, and re-layouts, on_device(): return jnp.stack(results, axis=1)  12.1 us
  transfers between devices with their start and end apart: 6, of which 6 were waited for; matrix products, arithmetic and copies ran while one was open for 6% of the time, Pallas kernels for 0%

commit v1 on v0

--- a/solution.py
+++ b/solution.py
@@ -23,7 +23,12 @@
     amplitudes = (integrals / divisor).astype(jnp.bfloat16)
     return jnp.dot(
         right_block,
-        lax.all_gather(amplitudes, "aux", axis=0, tiled=True),
+        jnp.concatenate(
+            lax.all_to_all(
+                jnp.stack([amplitudes for _ in range(lax.axis_size("aux"))]), "aux", 0, 0
+            ),
+            axis=0,
+        ),
         preferred_element_type=jnp.float32,
     )
 

time: 428 us -> 427 us (level)
  waiting for transfers between devices: 344 us -> 279 us
  blocking collectives: 0 us -> 57 us
  starting transfers between devices: 5.79 us -> 10.4 us
    all_gather x2 -> x0, waiting for transfers between devices: 110 us -> none  [pair_density(): lax.all_gather(amplitudes, 'aux', axis=0, tiled=True)]
    all_to_all x0 -> x1, blocking collectives: none -> 57 us  [pair_density(): lax.all_to_all(jnp.stack([amplitudes for _ in range(lax.axis_size('aux'))...]
    all_to_all x0 -> x1, waiting for transfers between devices: none -> 45.6 us  [pair_density(): lax.all_to_all(jnp.stack([amplitudes for _ in range(lax.axis_size('aux'))...]
    all_to_all x0 -> x1, starting transfers between devices: none -> 4.91 us  [pair_density(): lax.all_to_all(jnp.stack([amplitudes for _ in range(lax.axis_size('aux'))...]
  transfers between devices with their start and end apart: 6 -> 5, of which waited for: 6 -> 5; matrix products, arithmetic and copies ran while one was open for 6% -> 6% of each run, Pallas kernels for 0% -> 0%
where the time goes in v1:
time: 427 us; the launch traced here: 426 us
  waiting for transfers between devices  279 us (65%)
  blocking collectives  57 us (13%)
  matrix products  33.5 us (8%)
  local copies, waits for them, and re-layouts  28.2 us (7%)
  between operations  16 us (4%)
  starting transfers between devices  10.4 us (2%)
    reduce_scatter x2, waiting for transfers between devices, pair_density(): lax.psum_scatter(lax.dot_general(right_block, left_block, (((0,), (0,)),...  181 us
    all_to_all x1, blocking collectives, pair_density(): lax.all_to_all(jnp.stack([amplitudes for _ in range(lax.axis_size('aux'))...  57 us
    ppermute x2, waiting for transfers between devices, shifted(): return lax.ppermute(block, axis, route)  52.2 us
    all_to_all x1, waiting for transfers between devices, pair_density(): lax.all_to_all(jnp.stack([amplitudes for _ in range(lax.axis_size('aux'))...  45.6 us
    dot_general x2, matrix products, pair_density(): jnp.dot(right_block, jnp.concatenate(lax.all_to_all(jnp.stack([amplitudes...  18.9 us
    dot_general x2, matrix products, pair_density(): lax.dot_general(right_block, left_block, (((0,), (0,)), ((), ())), prefer...  14.5 us
    another operation x1, local copies, waits for them, and re-layouts, on_device(): return jnp.stack(results, axis=1)  12.1 us
  transfers between devices with their start and end apart: 5, of which 5 were waited for; matrix products, arithmetic and copies ran while one was open for 6% of the time, Pallas kernels for 0%

profile of v1, /device:TPU:1, one launch (start us, length us, event | category | flops | bytes accessed | tf_op | source)
XLA Modules:
  0.0 426.0 jit_solution(16285125298545256216)
XLA Ops:
  6.5 0.0 copy-start
  6.5 0.0 reduce-scatter.3.cloned.1.call-start
  6.5 3.0 collective-permute-start
  9.6 26.1 %collective-permute-done = bf16[768,1,1536]{2,0,1:T(8,128)(2,1)S(1)} collective-permute-done((bf16[768,1,1536]{2,0,1:T(8,128)(2,1)}, bf16[768,1,1536]{2,0,1:T(8,128)(2,1)S(1)}, u32[]{:S(2)}, u32[]{:S(2)}) %collective-permute-start) | collective-permute-done | bytes 2359328 | tf_op jit(solution)/shard_map/ppermute | solution.py:10
  35.7 0.0 copy-start.4
  35.7 1.4 copy-done.4
  37.1 7.9 %fusion.4 = f32[1536,1536]{1,0:T(8,128)} fusion(bf16[768,1,1536]{2,0,1:T(8,128)(2,1)} %param.5, bf16[768,1,1536]{2,0,1:T(8,128)(2,1)S(1)} %collective-permute-done), kind=kOutput, calls=%fused_computation.7 | convolution fusion | flops 3623878656 | bytes 14155776 | tf_op jit(solution)/shard_map/dot_general | solution.py:15
  45.0 0.0 copy-start.3
  45.0 0.0 reduce-scatter.3.cloned.1.call-update
  45.0 0.0 reduce-scatter.5.cloned.1.call-start
  45.1 2.5 collective-permute-start.1
  47.5 26.1 %collective-permute-done.1 = bf16[768,1,1536]{2,0,1:T(8,128)(2,1)S(1)} collective-permute-done((bf16[768,1,1536]{2,0,1:T(8,128)(2,1)}, bf16[768,1,1536]{2,0,1:T(8,128)(2,1)S(1)}, u32[]{:S(2)}, u32[]{:S(2)}) %collective-permute-start.1) | collective-permute-done | bytes 2359328 | tf_op jit(solution)/shard_map/ppermute | solution.py:10
  73.7 0.0 copy-start.6
  73.7 1.4 copy-done.6
  75.0 0.0 copy-done.3
  75.0 6.6 %fusion.1 = f32[1536,1536]{1,0:T(8,128)} fusion(bf16[768,1,1536]{2,0,1:T(8,128)(2,1)S(1)} %collective-permute-done.1, bf16[768,1,1536]{2,0,1:T(8,128)(2,1)S(1)} %copy-done.3), kind=kOutput, calls=%fused_computation.4 | convolution fusion | flops 3623878656 | bytes 14155776 | tf_op jit(solution)/shard_map/dot_general | solution.py:15
  81.6 0.0 copy-start.7
  81.6 0.0 copy-start.1
  81.6 0.0 copy-start.2
  81.6 0.0 reduce-scatter.5.cloned.1.call-update
  81.7 0.6 copy-done.7
  82.3 0.0 copy-done.1
  82.3 0.7 gather_fusion
  83.0 0.6 fusion.9
  86.1 0.0 copy-done.2
  86.1 0.0 copy-done
  86.1 8.4 %gather_fusion.1 = f32[1536]{0:T(1024)S(1)} fusion(f32[3072]{0:T(1024)S(1)} %copy-done, s32[2048]{0:T(1024)S(1)} %pad_clamp_fusion), kind=kCustom, calls=%fused_computation.1 | custom fusion | bytes 18432 | tf_op jit(solution)/shard_map/jit(_take)/gather | solution.py:45
  94.6 0.1 dynamic-slice_subtract_fusion
  94.6 80.0 %reduce-scatter.3.cloned.1.call-done = f32[192,1536]{1,0:T(8,128)} async-done(((f32[1536,1536]{1,0:T(8,128)}), f32[192,1536]{1,0:T(8,128)}) %reduce-scatter.3.cloned.1.call-update) | async-done | bytes 1179664 | tf_op jit(solution)/shard_map/reduce_scatter | solution.py:14
  174.6 100.9 %reduce-scatter.5.cloned.1.call-done = f32[192,1536]{1,0:T(8,128)} async-done(((f32[1536,1536]{1,0:T(8,128)}), f32[192,1536]{1,0:T(8,128)}) %reduce-scatter.5.cloned.1.call-update) | async-done | bytes 1179664 | tf_op jit(solution)/shard_map/reduce_scatter | solution.py:14
  275.5 2.0 divide_convert_fusion
  277.5 0.4 stack.6
  278.0 57.0 %all_to_all.10 = bf16[8,192,1536]{2,1,0:T(8,128)(2,1)} all-to-all(bf16[8,192,1536]{2,1,0:T(8,128)(2,1)S(1)} %stack.6), channel_id=1, replica_groups=mesh['aux'=8,'occ'=32] {'aux'}, dimensions={0} | all-to-all | bytes 9437184 | tf_op jit(solution)/shard_map/all_to_all | solution.py:27
  335.0 2.6 stack.7
  337.6 0.0 copy-start.5
  337.6 4.9 %all-to-all-start.1 = ((bf16[8,192,1536]{2,1,0:T(8,128)(2,1)}), bf16[8,192,1536]{2,1,0:T(8,128)(2,1)}, u32[]{:S(2)}, u32[]{:S(2)}) async-start(bf16[8,192,1536]{2,1,0:T(8,128)(2,1)} %stack.7), calls=%async_computation.3 | async-start | bytes 9437184 | tf_op jit(solution)/shard_map/all_to_all | solution.py:27
  342.5 0.0 copy-done.5
  342.5 8.4 %fusion.6 = f32[1536,768]{1,0:T(8,128)} fusion(bf16[1536,1536]{1,0:T(8,128)(2,1)} %bitcast.25, bf16[768,1,1536]{2,0,1:T(8,128)(2,1)S(1)} %copy-done.5), kind=kOutput, calls=%fused_computation.9 | convolution fusion | flops 3623878656 | bytes 11796480 | tf_op jit(solution)/shard_map/dot_general | solution.py:24
  351.0 45.6 %all-to-all-done.1 = bf16[8,192,1536]{2,1,0:T(8,128)(2,1)} async-done(((bf16[8,192,1536]{2,1,0:T(8,128)(2,1)}), bf16[8,192,1536]{2,1,0:T(8,128)(2,1)}, u32[]{:S(2)}, u32[]{:S(2)}) %all-to-all-start.1) | async-done | bytes 4718624 | tf_op jit(solution)/shard_map/all_to_all | solution.py:27
  396.6 10.5 %add_bitcast_fusion = f32[768,1,1536]{0,2,1:T(8,128)} fusion(f32[1536,768]{1,0:T(8,128)} %fusion.6, bf16[1536,1536]{1,0:T(8,128)(2,1)} %bitcast.6, bf16[768,1,1536]{2,0,1:T(8,128)(2,1)} %copy-done.6), kind=kOutput, calls=%fused_computation.2 | convolution fusion | flops 3625058304 | bytes 16515072 | tf_op jit(solution)/shard_map/dot_general | solution.py:24
  407.1 12.1 %copy.7 = f32[768,1,1536]{2,1,0:T(1,128)} copy(f32[768,1,1536]{0,2,1:T(8,128)} %add_bitcast_fusion) | data formatting | bytes 9437184 | tf_op jit(solution)/shard_map/stack | solution.py:62
  (6 shorter events, 0.0 us)
Async XLA Ops:
  6.5 79.6 %copy-start = (f32[3072]{0:T(1024)S(1)}, f32[3072]{0:T(1024)}, u32[]{:S(2)}) copy-start(f32[3072]{0:T(1024)} %param.7) | copy-start | bytes 36868
  6.5 168.1 %reduce-scatter.3.cloned.1.call-start = ((), (), s32[]{:S(2)}) async-start(), calls=%async_computation.4 | async-start | bytes 10616832 | tf_op jit(solution)/shard_map/reduce_scatter | solution.py:14
  6.5 29.1 %collective-permute-start = (bf16[768,1,1536]{2,0,1:T(8,128)(2,1)}, bf16[768,1,1536]{2,0,1:T(8,128)(2,1)S(1)}, u32[]{:S(2)}, u32[]{:S(2)}) collective-permute-start(bf16[768,1,1536]{2,0,1:T(8,128)(2,1)} %param.5), channel_id=1, source_target_pairs={{31,0},{0,1},{1,2},{2,3},{3,4},{4,5},{5,6},{6,7},{7,8},{8,9},{9,10... | collective-permute-start | bytes 7077896 | tf_op jit(solution)/shard_map/ppermute | solution.py:10
  35.7 1.4 copy-start.4
  45.0 30.0 %copy-start.3 = (bf16[768,1,1536]{2,0,1:T(8,128)(2,1)S(1)}, bf16[768,1,1536]{2,0,1:T(8,128)(2,1)}, u32[]{:S(2)}) copy-start(bf16[768,1,1536]{2,0,1:T(8,128)(2,1)} %param.5) | copy-start | bytes 7077892
  45.0 230.5 %reduce-scatter.5.cloned.1.call-start = ((), (), s32[]{:S(2)}) async-start(), calls=%async_computation.5 | async-start | bytes 10616832 | tf_op jit(solution)/shard_map/reduce_scatter | solution.py:14
  45.1 28.6 %collective-permute-start.1 = (bf16[768,1,1536]{2,0,1:T(8,128)(2,1)}, bf16[768,1,1536]{2,0,1:T(8,128)(2,1)S(1)}, u32[]{:S(2)}, u32[]{:S(2)}) collective-permute-start(bf16[768,1,1536]{2,0,1:T(8,128)(2,1)} %copy-done.4), channel_id=1, source_target_pairs={{31,0},{0,1},{1,2},{2,3},{3,4},{4,5},{5,6},{6,7},{7,8},{8,9},{9,10... | collective-permute-start | bytes 7077896 | tf_op jit(solution)/shard_map/ppermute | solution.py:10
  73.7 1.4 copy-start.6
  81.6 0.7 copy-start.7
  81.6 0.7 copy-start.1
  81.6 4.5 %copy-start.2 = (s32[1536]{0:T(1024)S(1)}, s32[1536]{0:T(1024)}, u32[]{:S(2)}) copy-start(s32[1536]{0:T(1024)} %param.9) | copy-start | bytes 18436
  337.6 4.9 %copy-start.5 = (bf16[768,1,1536]{2,0,1:T(8,128)(2,1)S(1)}, bf16[768,1,1536]{2,0,1:T(8,128)(2,1)}, u32[]{:S(2)}) copy-start(bf16[768,1,1536]{2,0,1:T(8,128)(2,1)} %copy-done.4) | copy-start | bytes 7077892
  337.6 59.0 %all-to-all-start.1 = ((bf16[8,192,1536]{2,1,0:T(8,128)(2,1)}), bf16[8,192,1536]{2,1,0:T(8,128)(2,1)}, u32[]{:S(2)}, u32[]{:S(2)}) async-start(bf16[8,192,1536]{2,1,0:T(8,128)(2,1)} %stack.7), calls=%async_computation.3 | async-start | bytes 9437184 | tf_op jit(solution)/shard_map/all_to_all | solution.py:27
Sparse Core Ops, SparseCore 0:
  45.2 129.3 reduce-scatter.2
  177.2 98.3 reduce-scatter.4
